TPU v7x, 32 devices: a whole 2x2x4 slice. The times are simulated.
32 devices in a mesh: tx: 8 (over z, x), ty: 4 (over y, core).
Axes of the slice: x: 2, y: 2, z: 4, core: 2. Of those that a mesh axis runs over, the one named last changes fastest.
Arguments:
- dynamics_residual: float32 [6, 48, 48, 16], P(None, 'tx', 'ty'), may hold values from -6 to 6
- density: float32 [6, 48, 48, 16], P(None, 'tx', 'ty'), may hold values from 0.5 to 8
- diagonal_gain: float32 [6, 48, 48, 16], P(None, 'tx', 'ty'), may hold values from 0.05 to 2
- vertical_coupling: float32 [6, 48, 48, 16], P(None, 'tx', 'ty'), may hold values from 0.2 to 8
- edge_panel: int32 [6, 4], replicated, may hold values from 0 to 5, as said below
- edge_side: int32 [6, 4], replicated, may hold values from 0 to 3, as said below
- edge_flip: int32 [6, 4], replicated, may hold values from 0 to 1, as said below
Outputs:
- solution: float32 [6, 48, 48, 16], P(None, 'tx', 'ty')
- coarse_correction: float32 [6, 24, 24, 16], P(None, 'tx', 'ty')
Inputs may be any that keep to these rules, and one draw needn't show every extreme that they name: The six panels are the faces of a cube, each with its own orientation and label: side s of panel p borders side edge_side[p, s] of panel edge_panel[p, s], the pairing is mutual, and no side borders a side of its own panel. `edge_side`: see edge_panel. `edge_flip`: equal on both sides of a bordering pair.
All inputs are finite; a program needn't handle non-finite values.
Results may differ from a plain program's by a relative error of at most 0.00005.
Values sent between devices are 32-bit elements; how exact they have to be, the bound alone decides.
A program may use at most 64 MiB of HBM per device.

v0:
```python
import jax
import jax.numpy as jnp
from jax import lax
from jax.sharding import PartitionSpec as P

relaxation = 0.8
highest = lax.Precision.HIGHEST


def extended(x, sides, width):
    for axis, dim in sides:
        count, length = (lax.axis_size(axis), x.shape[dim])
        up = [(i, (i + 1) % count) for i in range(count - 1)]
        down = [(j, i) for i, j in up]
        last = lax.slice_in_dim(x, length - width, length, axis=dim)
        first = lax.slice_in_dim(x, 0, width, axis=dim)
        before = lax.ppermute(last, axis, up)
        after = lax.ppermute(first, axis, down)
        x = jnp.concatenate([before, x, after], axis=dim)
    return x


def partner(value, axis, distance):
    mask = 2**distance
    pairs = [(source, source ^ mask) for source in range(lax.axis_size(axis))]
    return lax.ppermute(value, axis, pairs)


def lower_levels(values):
    return jnp.concatenate([jnp.zeros_like(values[..., :1]), values[..., :-1]], axis=-1)


def upper_levels(values):
    return jnp.concatenate([values[..., 1:], jnp.zeros_like(values[..., :1])], axis=-1)


def vertical_part(grid_field, vertical):
    return vertical * (grid_field - upper_levels(grid_field)) + lower_levels(vertical) * (
        grid_field - lower_levels(grid_field)
    )


def diagonal_of(cell_gain, vertical, horizontal):
    return cell_gain + 4.0 * horizontal + vertical + lower_levels(vertical)


def neighbour_sum(padded):
    return padded[:, :-2, 1:-1] + padded[:, 2:, 1:-1] + padded[:, 1:-1, :-2] + padded[:, 1:-1, 2:]


def apply_operator(grid_field, padded, cell_gain, vertical, horizontal):
    return (
        cell_gain * grid_field
        + horizontal * (4.0 * grid_field - neighbour_sum(padded))
        + vertical_part(grid_field, vertical)
    )


def restrict(values):
    shaped = values.reshape(
        values.shape[0], values.shape[1] // 2, 2, values.shape[2] // 2, 2, values.shape[3]
    )
    return shaped.mean(axis=(2, 4))


def prolong(values):
    return jnp.repeat(jnp.repeat(values, 2, axis=1), 2, axis=2)


def window_piece(held_block, positions, offset):
    length = held_block.shape[2]
    local_index = positions - offset
    inside = ((local_index >= 0) & (local_index < length)).astype(jnp.float32)
    picked = jnp.take(held_block, jnp.clip(local_index, 0, length - 1), axis=2)
    return picked * inside[None, None, :, None]


def select_rims(forward, mirrored, edge_panel, edge_side, edge_flip, first_side):
    side_codes = edge_side[:, first_side : first_side + 2]
    panel_codes = edge_panel[:, first_side : first_side + 2]
    flip_codes = edge_flip[:, first_side : first_side + 2].astype(jnp.float32)
    matched = (
        (side_codes[:, :, None, None] == jnp.arange(4)[None, None, :, None])
        & (panel_codes[:, :, None, None] == jnp.arange(6)[None, None, None, :])
    ).astype(jnp.float32)
    straight = matched * (1.0 - flip_codes)[:, :, None, None]
    turned = matched * flip_codes[:, :, None, None]
    return jnp.einsum("pstq,tqjl->psjl", straight, forward, precision=highest) + jnp.einsum(
        "pstq,tqjl->psjl", turned, mirrored, precision=highest
    )


def padded_tile(grid_field, edge_panel, edge_side, edge_flip):
    row_index = lax.axis_index("tx")
    col_index = lax.axis_index("ty")
    row_count = lax.axis_size("tx")
    col_count = lax.axis_size("ty")
    tile_rows = grid_field.shape[1]
    tile_cols = grid_field.shape[2]
    side_cells = tile_rows * row_count
    padded = extended(grid_field, (("tx", 1), ("ty", 2)), 1)
    across_mask = jnp.stack([row_index == 0, row_index == row_count - 1]).astype(jnp.float32)
    along_mask = jnp.stack([col_index == 0, col_index == col_count - 1]).astype(jnp.float32)
    row_sides = jnp.stack([grid_field[:, 0], grid_field[:, -1]]) * across_mask[:, None, None, None]
    col_sides = (
        jnp.stack([grid_field[:, :, 0], grid_field[:, :, -1]]) * along_mask[:, None, None, None]
    )
    col_block = lax.psum(row_sides, "tx")
    row_block = lax.psum(col_sides, "ty")
    col_positions = col_index * tile_cols + jnp.arange(tile_cols)
    row_positions = row_index * tile_rows + jnp.arange(tile_rows)
    cross_cols = jnp.stack(
        [
            window_piece(row_block, col_positions, row_index * tile_rows),
            window_piece(row_block, side_cells - 1 - col_positions, row_index * tile_rows),
        ]
    )
    summed_cols = lax.psum(cross_cols, "tx")
    cross_rows = jnp.stack(
        [
            window_piece(col_block, row_positions, col_index * tile_cols),
            window_piece(col_block, side_cells - 1 - row_positions, col_index * tile_cols),
        ]
    )
    summed_rows = lax.psum(cross_rows, "ty")
    mirror_rowblock = row_block[:, :, ::-1]
    for bit in range(row_count.bit_length() - 1):
        mirror_rowblock = partner(mirror_rowblock, "tx", bit)
    mirror_colblock = col_block[:, :, ::-1]
    for bit in range(col_count.bit_length() - 1):
        mirror_colblock = partner(mirror_colblock, "ty", bit)
    cols_forward = jnp.concatenate([col_block, summed_cols[0]], axis=0)
    cols_mirror = jnp.concatenate([mirror_colblock, summed_cols[1]], axis=0)
    rows_forward = jnp.concatenate([summed_rows[0], row_block], axis=0)
    rows_mirror = jnp.concatenate([summed_rows[1], mirror_rowblock], axis=0)
    col_rims = select_rims(cols_forward, cols_mirror, edge_panel, edge_side, edge_flip, 0)
    row_rims = select_rims(rows_forward, rows_mirror, edge_panel, edge_side, edge_flip, 2)
    top_rim = jnp.where(row_index == 0, col_rims[:, 0], padded[:, 0, 1:-1])
    bottom_rim = jnp.where(row_index == row_count - 1, col_rims[:, 1], padded[:, -1, 1:-1])
    left_rim = jnp.where(col_index == 0, row_rims[:, 0], padded[:, 1:-1, 0])
    right_rim = jnp.where(col_index == col_count - 1, row_rims[:, 1], padded[:, 1:-1, -1])
    padded = padded.at[:, 0, 1:-1].set(top_rim)
    padded = padded.at[:, -1, 1:-1].set(bottom_rim)
    padded = padded.at[:, 1:-1, 0].set(left_rim)
    padded = padded.at[:, 1:-1, -1].set(right_rim)
    return padded


def shards(
    dynamics_residual, density, diagonal_gain, vertical_coupling, edge_panel, edge_side, edge_flip
):
    right_side = density * dynamics_residual
    fine_diagonal = diagonal_of(diagonal_gain, vertical_coupling, 1.0)
    smoothed = relaxation * right_side / fine_diagonal
    applied = apply_operator(
        smoothed,
        padded_tile(smoothed, edge_panel, edge_side, edge_flip),
        diagonal_gain,
        vertical_coupling,
        1.0,
    )
    coarse_rhs = restrict(right_side - applied)
    coarse_gain = restrict(diagonal_gain)
    coarse_vertical = restrict(vertical_coupling)
    coarse_diagonal = diagonal_of(coarse_gain, coarse_vertical, 0.25)
    coarse_guess = relaxation * coarse_rhs / coarse_diagonal
    coarse_applied = apply_operator(
        coarse_guess,
        padded_tile(coarse_guess, edge_panel, edge_side, edge_flip),
        coarse_gain,
        coarse_vertical,
        0.25,
    )
    coarse_correction = coarse_guess + relaxation * (coarse_rhs - coarse_applied) / coarse_diagonal
    corrected = smoothed + prolong(coarse_correction)
    final_applied = apply_operator(
        corrected,
        padded_tile(corrected, edge_panel, edge_side, edge_flip),
        diagonal_gain,
        vertical_coupling,
        1.0,
    )
    solution = corrected + relaxation * (right_side - final_applied) / fine_diagonal
    return (solution, coarse_correction)


def solution(mesh):
    placed = (
        P(None, "tx", "ty", None),
        P(None, "tx", "ty", None),
        P(None, "tx", "ty", None),
        P(None, "tx", "ty", None),
        P(),
        P(),
        P(),
    )
    return jax.shard_map(
        shards,
        mesh=mesh,
        in_specs=placed,
        out_specs=(P(None, "tx", "ty", None), P(None, "tx", "ty", None)),
        check_vma=False,
    )
```

profile of v0, /device:TPU:0, one launch (start us, length us, event | category | flops | bytes accessed | tf_op | source)
XLA Modules:
  0.0 281.6 jit_solution(7349908816677631455)
XLA Ops:
  3.6 13.3 %psum.85 = f32[2,6,6,16]{3,1,0,2:T(8,128)S(1)} all-reduce(f32[2,6,6,16]{3,1,0,2:T(8,128)S(1)} %maximum_multiply_fusion.2), channel_id=1, replica_groups=mesh['tx'=8,'ty'=4] {'ty'}, use_global_device_ids=true, to_apply=%region_1.0 | all-reduce | flops 1152 | bytes 9216 | tf_op jit(solution)/shard_map/psum | solution.py:109
  19.8 4.5 %collective-permute-start = (f32[6,1,12,16]{3,0,2,1:T(8,128)S(1)}, f32[6,1,12,16]{3,0,2,1:T(8,128)S(1)}, u32[]{:S(2)}, u32[]{:S(2)}) collective-permute-start(f32[6,1,12,16]{3,0,2,1:T(8,128)S(1)} %get-tuple-element.193), channel_id=1, source_target_pairs={{0,4},{4,8},{8,12},{12,16},{16,20},{20,24},{24,28},{1,5},{5,9},{9,... | collective-permute-start | bytes 13832 | tf_op jit(solution)/shard_map/ppermute | solution.py:17
  25.9 38.7 %all-reduce.10 = (f32[2,2,6,12,16]{4,2,1,3,0:T(8,128)S(1)}, f32[2,6,12,16]{3,1,0,2:T(8,128)S(1)}) all-reduce(f32[2,2,6,12,16]{4,2,1,3,0:T(8,128)S(1)} %pad_maximum_fusion.2, f32[2,6,12,16]{3,1,0,2:T(8,128)S(1)} %copy.51), channel_id=1, replica_groups=mesh['tx'=8,'ty'=4] {'tx'}, use_global_device_ids=true, to_apply=%region_2.4 | all-reduce | flops 6912 | bytes 55296 | tf_op jit(solution)/shard_map/psum | solution.py:118
  69.0 11.5 %psum.87 = f32[2,2,6,6,16]{4,2,1,3,0:T(8,128)S(1)} all-reduce(f32[2,2,6,6,16]{4,2,1,3,0:T(8,128)S(1)} %pad_maximum_fusion.5), channel_id=1, replica_groups=mesh['tx'=8,'ty'=4] {'ty'}, use_global_device_ids=true, to_apply=%region_3.6 | all-reduce | flops 2304 | bytes 18432 | tf_op jit(solution)/shard_map/psum | solution.py:125
  81.6 2.0 collective-permute-start.2
  85.3 3.7 %collective-permute-done.7 = f32[2,6,6,16]{3,1,0,2:T(8,128)S(1)} collective-permute-done((f32[2,6,6,16]{3,1,0,2:T(8,128)S(1)}, f32[2,6,6,16]{3,1,0,2:T(8,128)S(1)}, u32[]{:S(2)}, u32[]{:S(2)}) %collective-permute-start.7) | collective-permute-done | bytes 4640 | tf_op jit(solution)/shard_map/ppermute | solution.py:26
  89.2 4.0 %collective-permute-start.5 = (f32[2,6,12,16]{3,1,0,2:T(8,128)S(1)}, f32[2,6,12,16]{3,1,0,2:T(8,128)S(1)}, u32[]{:S(2)}, u32[]{:S(2)}) collective-permute-start(f32[2,6,12,16]{3,1,0,2:T(8,128)S(1)} %collective-permute-done.4), channel_id=1, source_target_pairs={{0,2},{1,3},{2,0},{3,1},{4,6},{5,7},{6,4},{7,5},{8,10},{9,11},{10,... | collective-permute-start | bytes 27656 | tf_op jit(solution)/shard_map/ppermute | solution.py:26
  93.1 2.0 collective-permute-done.8
  98.8 10.7 %psum.89 = f32[2,6,3,16]{3,1,0,2:T(8,128)S(1)} all-reduce(f32[2,6,3,16]{3,1,0,2:T(8,128)S(1)} %maximum_multiply_fusion.4), channel_id=1, replica_groups=mesh['tx'=8,'ty'=4] {'ty'}, use_global_device_ids=true, to_apply=%region_8.11 | all-reduce | flops 576 | bytes 4608 | tf_op jit(solution)/shard_map/psum | solution.py:109
  111.0 37.9 %all-reduce.9 = (f32[2,2,6,6,16]{4,2,1,3,0:T(8,128)S(1)}, f32[2,6,6,16]{3,1,0,2:T(8,128)S(1)}) all-reduce(f32[2,2,6,6,16]{4,2,1,3,0:T(8,128)S(1)} %pad_maximum_fusion.6, f32[2,6,6,16]{3,1,0,2:T(8,128)S(1)} %copy.60), channel_id=1, replica_groups=mesh['tx'=8,'ty'=4] {'tx'}, use_global_device_ids=true, to_apply=%region_9.13 | all-reduce | flops 3456 | bytes 27648 | tf_op jit(solution)/shard_map/psum | solution.py:118
  150.3 10.5 %psum.91 = f32[2,2,6,3,16]{4,2,1,3,0:T(8,128)S(1)} all-reduce(f32[2,2,6,3,16]{4,2,1,3,0:T(8,128)S(1)} %pad_maximum_fusion.8), channel_id=1, replica_groups=mesh['tx'=8,'ty'=4] {'ty'}, use_global_device_ids=true, to_apply=%region_10.15 | all-reduce | flops 1152 | bytes 9216 | tf_op jit(solution)/shard_map/psum | solution.py:125
  162.1 4.5 %collective-permute-start.9 = (f32[6,1,6,16]{3,0,2,1:T(8,128)S(1)}, f32[6,1,6,16]{3,0,2,1:T(8,128)S(1)}, u32[]{:S(2)}, u32[]{:S(2)}) collective-permute-start(f32[6,1,6,16]{3,0,2,1:T(8,128)S(1)} %get-tuple-element.213), channel_id=1, source_target_pairs={{0,4},{4,8},{8,12},{12,16},{16,20},{20,24},{24,28},{1,5},{5,9},{9,... | collective-permute-start | bytes 6920 | tf_op jit(solution)/shard_map/ppermute | solution.py:17
  170.8 1.8 collective-permute-start.16
  173.0 3.2 %collective-permute-start.13 = (f32[2,6,6,16]{3,1,0,2:T(8,128)S(1)}, f32[2,6,6,16]{3,1,0,2:T(8,128)S(1)}, u32[]{:S(2)}, u32[]{:S(2)}) collective-permute-start(f32[2,6,6,16]{3,1,0,2:T(8,128)S(1)} %rev.20), channel_id=1, source_target_pairs={{0,1},{1,0},{2,3},{3,2},{4,5},{5,4},{6,7},{7,6},{8,9},{9,8},{10,11... | collective-permute-start | bytes 13832 | tf_op jit(solution)/shard_map/ppermute | solution.py:26
  177.1 2.9 %collective-permute-start.14 = (f32[2,6,6,16]{3,1,0,2:T(8,128)S(1)}, f32[2,6,6,16]{3,1,0,2:T(8,128)S(1)}, u32[]{:S(2)}, u32[]{:S(2)}) collective-permute-start(f32[2,6,6,16]{3,1,0,2:T(8,128)S(1)} %collective-permute-done.13), channel_id=1, source_target_pairs={{0,2},{1,3},{2,0},{3,1},{4,6},{5,7},{6,4},{7,5},{8,10},{9,11},{10,... | collective-permute-start | bytes 13832 | tf_op jit(solution)/shard_map/ppermute | solution.py:26
  184.2 11.0 %psum.93 = f32[2,6,6,16]{3,1,0,2:T(8,128)S(1)} all-reduce(f32[2,6,6,16]{3,1,0,2:T(8,128)S(1)} %copy_multiply_fusion.3), channel_id=1, replica_groups=mesh['tx'=8,'ty'=4] {'ty'}, use_global_device_ids=true, to_apply=%region_12.17 | all-reduce | flops 1152 | bytes 9216 | tf_op jit(solution)/shard_map/psum | solution.py:109
  197.9 39.3 %all-reduce.8 = (f32[2,2,6,12,16]{4,2,1,3,0:T(8,128)S(1)}, f32[2,6,12,16]{3,1,0,2:T(8,128)S(1)}) all-reduce(f32[2,2,6,12,16]{4,2,1,3,0:T(8,128)S(1)} %pad_maximum_fusion.3, f32[2,6,12,16]{3,1,0,2:T(8,128)S(1)} %copy.67), channel_id=1, replica_groups=mesh['tx'=8,'ty'=4] {'tx'}, use_global_device_ids=true, to_apply=%region_13.18 | all-reduce | flops 6912 | bytes 55296 | tf_op jit(solution)/shard_map/psum | solution.py:118
  238.8 11.1 %psum.95 = f32[2,2,6,6,16]{4,2,1,3,0:T(8,128)S(1)} all-reduce(f32[2,2,6,6,16]{4,2,1,3,0:T(8,128)S(1)} %pad_maximum_fusion.7), channel_id=1, replica_groups=mesh['tx'=8,'ty'=4] {'ty'}, use_global_device_ids=true, to_apply=%region_14.19 | all-reduce | flops 2304 | bytes 18432 | tf_op jit(solution)/shard_map/psum | solution.py:125
  252.0 4.7 %collective-permute-start.18 = (f32[6,1,12,16]{3,0,2,1:T(8,128)S(1)}, f32[6,1,12,16]{3,0,2,1:T(8,128)S(1)}, u32[]{:S(2)}, u32[]{:S(2)}) collective-permute-start(f32[6,1,12,16]{3,0,2,1:T(8,128)S(1)} %copy-done.4), channel_id=1, source_target_pairs={{0,4},{4,8},{8,12},{12,16},{16,20},{20,24},{24,28},{1,5},{5,9},{9,... | collective-permute-start | bytes 13832 | tf_op jit(solution)/shard_map/ppermute | solution.py:17
  258.5 1.6 collective-permute-start.20
  261.4 4.4 %collective-permute-start.25 = (f32[2,6,6,16]{3,1,0,2:T(8,128)}, f32[2,6,6,16]{3,1,0,2:T(8,128)}, u32[]{:S(2)}, u32[]{:S(2)}) collective-permute-start(f32[2,6,6,16]{3,1,0,2:T(8,128)} %collective-permute-done.24), channel_id=1, source_target_pairs={{0,8},{4,12},{8,0},{12,4},{16,24},{20,28},{24,16},{28,20},{1,9},{5... | collective-permute-start | bytes 13832 | tf_op jit(solution)/shard_map/ppermute | solution.py:26
  267.6 3.3 %collective-permute-start.22 = (f32[2,6,12,16]{3,1,0,2:T(8,128)}, f32[2,6,12,16]{3,1,0,2:T(8,128)S(1)}, u32[]{:S(2)}, u32[]{:S(2)}) collective-permute-start(f32[2,6,12,16]{3,1,0,2:T(8,128)} %rev.22), channel_id=1, source_target_pairs={{0,1},{1,0},{2,3},{3,2},{4,5},{5,4},{6,7},{7,6},{8,9},{9,8},{10,11... | collective-permute-start | bytes 27656 | tf_op jit(solution)/shard_map/ppermute | solution.py:26
  272.0 2.3 collective-permute-start.23
  274.3 2.6 collective-permute-done.26
  (215 shorter events, 48.0 us)
Async XLA Ops:
  16.9 68.0 %collective-permute-start.6 = (f32[2,6,6,16]{3,1,0,2:T(8,128)S(1)}, f32[2,6,6,16]{3,1,0,2:T(8,128)S(1)}, u32[]{:S(2)}, u32[]{:S(2)}) collective-permute-start(f32[2,6,6,16]{3,1,0,2:T(8,128)S(1)} %rev.19), channel_id=1, source_target_pairs={{0,4},{4,0},{8,12},{12,8},{16,20},{20,16},{24,28},{28,24},{1,5},{5... | collective-permute-start | bytes 13832 | tf_op jit(solution)/shard_map/ppermute | solution.py:26
  18.5 63.1 %collective-permute-start.1 = (f32[6,1,12,16]{3,0,2,1:T(8,128)S(1)}, f32[6,1,12,16]{3,0,2,1:T(8,128)S(1)}, u32[]{:S(2)}, u32[]{:S(2)}) collective-permute-start(f32[6,1,12,16]{3,0,2,1:T(8,128)S(1)} %get-tuple-element.192), channel_id=1, source_target_pairs={{4,0},{8,4},{12,8},{16,12},{20,16},{24,20},{28,24},{5,1},{9,5},{13... | collective-permute-start | bytes 13832 | tf_op jit(solution)/shard_map/ppermute | solution.py:18
  19.8 61.8 %collective-permute-start = (f32[6,1,12,16]{3,0,2,1:T(8,128)S(1)}, f32[6,1,12,16]{3,0,2,1:T(8,128)S(1)}, u32[]{:S(2)}, u32[]{:S(2)}) collective-permute-start(f32[6,1,12,16]{3,0,2,1:T(8,128)S(1)} %get-tuple-element.193), channel_id=1, source_target_pairs={{0,4},{4,8},{8,12},{12,16},{16,20},{20,24},{24,28},{1,5},{5,9},{9,... | collective-permute-start | bytes 13832 | tf_op jit(solution)/shard_map/ppermute | solution.py:17
  64.7 24.5 %collective-permute-start.4 = (f32[2,6,12,16]{3,1,0,2:T(8,128)S(1)}, f32[2,6,12,16]{3,1,0,2:T(8,128)S(1)}, u32[]{:S(2)}, u32[]{:S(2)}) collective-permute-start(f32[2,6,12,16]{3,1,0,2:T(8,128)S(1)} %rev.18), channel_id=1, source_target_pairs={{0,1},{1,0},{2,3},{3,2},{4,5},{5,4},{6,7},{7,6},{8,9},{9,8},{10,11... | collective-permute-start | bytes 27656 | tf_op jit(solution)/shard_map/ppermute | solution.py:26
  81.6 7.5 %collective-permute-start.2 = (f32[6,8,1,16]{3,0,1,2:T(8,128)S(1)}, f32[6,8,1,16]{3,0,1,2:T(8,128)S(1)}, u32[]{:S(2)}, u32[]{:S(2)}) collective-permute-start(f32[6,8,1,16]{3,0,1,2:T(8,128)S(1)} %get-tuple-element.178), channel_id=1, source_target_pairs={{0,1},{1,2},{2,3},{4,5},{5,6},{6,7},{8,9},{9,10},{10,11},{12,13},{... | collective-permute-start | bytes 9224 | tf_op jit(solution)/shard_map/ppermute | solution.py:17
  83.6 5.5 %collective-permute-start.3 = (f32[6,8,1,16]{3,0,1,2:T(8,128)S(1)}, f32[6,8,1,16]{3,0,1,2:T(8,128)S(1)}, u32[]{:S(2)}, u32[]{:S(2)}) collective-permute-start(f32[6,8,1,16]{3,0,1,2:T(8,128)S(1)} %get-tuple-element.179), channel_id=1, source_target_pairs={{1,0},{2,1},{3,2},{5,4},{6,5},{7,6},{9,8},{10,9},{11,10},{13,12},{... | collective-permute-start | bytes 9224 | tf_op jit(solution)/shard_map/ppermute | solution.py:18
  89.1 6.0 %collective-permute-start.8 = (f32[2,6,6,16]{3,1,0,2:T(8,128)S(1)}, f32[2,6,6,16]{3,1,0,2:T(8,128)S(1)}, u32[]{:S(2)}, u32[]{:S(2)}) collective-permute-start(f32[2,6,6,16]{3,1,0,2:T(8,128)S(1)} %collective-permute-done.7), channel_id=1, source_target_pairs={{0,16},{4,20},{8,24},{12,28},{16,0},{20,4},{24,8},{28,12},{1,17},{... | collective-permute-start | bytes 13832 | tf_op jit(solution)/shard_map/ppermute | solution.py:26
  89.2 6.6 %collective-permute-start.5 = (f32[2,6,12,16]{3,1,0,2:T(8,128)S(1)}, f32[2,6,12,16]{3,1,0,2:T(8,128)S(1)}, u32[]{:S(2)}, u32[]{:S(2)}) collective-permute-start(f32[2,6,12,16]{3,1,0,2:T(8,128)S(1)} %collective-permute-done.4), channel_id=1, source_target_pairs={{0,2},{1,3},{2,0},{3,1},{4,6},{5,7},{6,4},{7,5},{8,10},{9,11},{10,... | collective-permute-start | bytes 27656 | tf_op jit(solution)/shard_map/ppermute | solution.py:26
  109.5 61.2 %collective-permute-start.15 = (f32[2,6,3,16]{3,1,0,2:T(8,128)S(1)}, f32[2,6,3,16]{3,1,0,2:T(8,128)S(1)}, u32[]{:S(2)}, u32[]{:S(2)}) collective-permute-start(f32[2,6,3,16]{3,1,0,2:T(8,128)S(1)} %rev.21), channel_id=1, source_target_pairs={{0,4},{4,0},{8,12},{12,8},{16,20},{20,16},{24,28},{28,24},{1,5},{5... | collective-permute-start | bytes 6920 | tf_op jit(solution)/shard_map/ppermute | solution.py:26
  160.8 6.3 %collective-permute-start.10 = (f32[6,1,6,16]{3,0,1,2:T(8,128)S(1)}, f32[6,1,6,16]{3,0,1,2:T(8,128)S(1)}, u32[]{:S(2)}, u32[]{:S(2)}) collective-permute-start(f32[6,1,6,16]{3,0,1,2:T(8,128)S(1)} %get-tuple-element.212), channel_id=1, source_target_pairs={{4,0},{8,4},{12,8},{16,12},{20,16},{24,20},{28,24},{5,1},{9,5},{13... | collective-permute-start | bytes 6920 | tf_op jit(solution)/shard_map/ppermute | solution.py:18
  162.1 6.1 %collective-permute-start.9 = (f32[6,1,6,16]{3,0,2,1:T(8,128)S(1)}, f32[6,1,6,16]{3,0,2,1:T(8,128)S(1)}, u32[]{:S(2)}, u32[]{:S(2)}) collective-permute-start(f32[6,1,6,16]{3,0,2,1:T(8,128)S(1)} %get-tuple-element.213), channel_id=1, source_target_pairs={{0,4},{4,8},{8,12},{12,16},{16,20},{20,24},{24,28},{1,5},{5,9},{9,... | collective-permute-start | bytes 6920 | tf_op jit(solution)/shard_map/ppermute | solution.py:17
  168.2 8.6 %collective-permute-start.11 = (f32[6,5,1,16]{3,0,1,2:T(8,128)S(1)}, f32[6,5,1,16]{3,0,1,2:T(8,128)S(1)}, u32[]{:S(2)}, u32[]{:S(2)}) collective-permute-start(f32[6,5,1,16]{3,0,1,2:T(8,128)S(1)} %get-tuple-element.200), channel_id=1, source_target_pairs={{0,1},{1,2},{2,3},{4,5},{5,6},{6,7},{8,9},{9,10},{10,11},{12,13},{... | collective-permute-start | bytes 5768 | tf_op jit(solution)/shard_map/ppermute | solution.py:17
  169.4 7.3 %collective-permute-start.12 = (f32[6,5,1,16]{3,0,1,2:T(8,128)S(1)}, f32[6,5,1,16]{3,0,1,2:T(8,128)S(1)}, u32[]{:S(2)}, u32[]{:S(2)}) collective-permute-start(f32[6,5,1,16]{3,0,1,2:T(8,128)S(1)} %get-tuple-element.201), channel_id=1, source_target_pairs={{1,0},{2,1},{3,2},{5,4},{6,5},{7,6},{9,8},{10,9},{11,10},{13,12},{... | collective-permute-start | bytes 5768 | tf_op jit(solution)/shard_map/ppermute | solution.py:18
  170.8 5.5 %collective-permute-start.16 = (f32[2,6,3,16]{3,1,0,2:T(8,128)S(1)}, f32[2,6,3,16]{3,1,0,2:T(8,128)S(1)}, u32[]{:S(2)}, u32[]{:S(2)}) collective-permute-start(f32[2,6,3,16]{3,1,0,2:T(8,128)S(1)} %collective-permute-done.15), channel_id=1, source_target_pairs={{0,8},{4,12},{8,0},{12,4},{16,24},{20,28},{24,16},{28,20},{1,9},{5... | collective-permute-start | bytes 6920 | tf_op jit(solution)/shard_map/ppermute | solution.py:26
  176.3 5.0 %collective-permute-start.17 = (f32[2,6,3,16]{3,1,0,2:T(8,128)S(1)}, f32[2,6,3,16]{3,1,0,2:T(8,128)S(1)}, u32[]{:S(2)}, u32[]{:S(2)}) collective-permute-start(f32[2,6,3,16]{3,1,0,2:T(8,128)S(1)} %collective-permute-done.16), channel_id=1, source_target_pairs={{0,16},{4,20},{8,24},{12,28},{16,0},{20,4},{24,8},{28,12},{1,17},{... | collective-permute-start | bytes 6920 | tf_op jit(solution)/shard_map/ppermute | solution.py:26
  177.1 5.0 %collective-permute-start.14 = (f32[2,6,6,16]{3,1,0,2:T(8,128)S(1)}, f32[2,6,6,16]{3,1,0,2:T(8,128)S(1)}, u32[]{:S(2)}, u32[]{:S(2)}) collective-permute-start(f32[2,6,6,16]{3,1,0,2:T(8,128)S(1)} %collective-permute-done.13), channel_id=1, source_target_pairs={{0,2},{1,3},{2,0},{3,1},{4,6},{5,7},{6,4},{7,5},{8,10},{9,11},{10,... | collective-permute-start | bytes 13832 | tf_op jit(solution)/shard_map/ppermute | solution.py:26
  238.5 22.9 %collective-permute-start.24 = (f32[2,6,6,16]{3,1,0,2:T(8,128)}, f32[2,6,6,16]{3,1,0,2:T(8,128)}, u32[]{:S(2)}, u32[]{:S(2)}) collective-permute-start(f32[2,6,6,16]{3,1,0,2:T(8,128)} %rev.23), channel_id=1, source_target_pairs={{0,4},{4,0},{8,12},{12,8},{16,20},{20,16},{24,28},{28,24},{1,5},{5... | collective-permute-start | bytes 13832 | tf_op jit(solution)/shard_map/ppermute | solution.py:26
  250.7 6.7 %collective-permute-start.19 = (f32[6,1,12,16]{3,0,1,2:T(8,128)S(1)}, f32[6,1,12,16]{3,0,1,2:T(8,128)S(1)}, u32[]{:S(2)}, u32[]{:S(2)}) collective-permute-start(f32[6,1,12,16]{3,0,1,2:T(8,128)S(1)} %copy-done.5), channel_id=1, source_target_pairs={{4,0},{8,4},{12,8},{16,12},{20,16},{24,20},{28,24},{5,1},{9,5},{13... | collective-permute-start | bytes 13832 | tf_op jit(solution)/shard_map/ppermute | solution.py:18
  252.0 6.5 %collective-permute-start.18 = (f32[6,1,12,16]{3,0,2,1:T(8,128)S(1)}, f32[6,1,12,16]{3,0,2,1:T(8,128)S(1)}, u32[]{:S(2)}, u32[]{:S(2)}) collective-permute-start(f32[6,1,12,16]{3,0,2,1:T(8,128)S(1)} %copy-done.4), channel_id=1, source_target_pairs={{0,4},{4,8},{8,12},{12,16},{16,20},{20,24},{24,28},{1,5},{5,9},{9,... | collective-permute-start | bytes 13832 | tf_op jit(solution)/shard_map/ppermute | solution.py:17
  258.5 12.4 %collective-permute-start.20 = (f32[6,8,1,16]{3,0,1,2:T(8,128)S(1)}, f32[6,8,1,16]{3,0,1,2:T(8,128)S(1)}, u32[]{:S(2)}, u32[]{:S(2)}) collective-permute-start(f32[6,8,1,16]{3,0,1,2:T(8,128)S(1)} %get-tuple-element.176), channel_id=1, source_target_pairs={{0,1},{1,2},{2,3},{4,5},{5,6},{6,7},{8,9},{9,10},{10,11},{12,13},{... | collective-permute-start | bytes 9224 | tf_op jit(solution)/shard_map/ppermute | solution.py:17
  260.1 10.8 %collective-permute-start.21 = (f32[6,8,1,16]{3,0,1,2:T(8,128)S(1)}, f32[6,8,1,16]{3,0,1,2:T(8,128)S(1)}, u32[]{:S(2)}, u32[]{:S(2)}) collective-permute-start(f32[6,8,1,16]{3,0,1,2:T(8,128)S(1)} %get-tuple-element.177), channel_id=1, source_target_pairs={{1,0},{2,1},{3,2},{5,4},{6,5},{7,6},{9,8},{10,9},{11,10},{13,12},{... | collective-permute-start | bytes 9224 | tf_op jit(solution)/shard_map/ppermute | solution.py:18
  261.4 9.5 %collective-permute-start.25 = (f32[2,6,6,16]{3,1,0,2:T(8,128)}, f32[2,6,6,16]{3,1,0,2:T(8,128)}, u32[]{:S(2)}, u32[]{:S(2)}) collective-permute-start(f32[2,6,6,16]{3,1,0,2:T(8,128)} %collective-permute-done.24), channel_id=1, source_target_pairs={{0,8},{4,12},{8,0},{12,4},{16,24},{20,28},{24,16},{28,20},{1,9},{5... | collective-permute-start | bytes 13832 | tf_op jit(solution)/shard_map/ppermute | solution.py:26
  270.9 6.0 %collective-permute-start.26 = (f32[2,6,6,16]{3,1,0,2:T(8,128)}, f32[2,6,6,16]{3,1,0,2:T(8,128)S(1)}, u32[]{:S(2)}, u32[]{:S(2)}) collective-permute-start(f32[2,6,6,16]{3,1,0,2:T(8,128)} %collective-permute-done.25), channel_id=1, source_target_pairs={{0,16},{4,20},{8,24},{12,28},{16,0},{20,4},{24,8},{28,12},{1,17},{... | collective-permute-start | bytes 13832 | tf_op jit(solution)/shard_map/ppermute | solution.py:26
  272.0 5.4 %collective-permute-start.23 = (f32[2,6,12,16]{3,1,0,2:T(8,128)S(1)}, f32[2,6,12,16]{3,1,0,2:T(8,128)S(1)}, u32[]{:S(2)}, u32[]{:S(2)}) collective-permute-start(f32[2,6,12,16]{3,1,0,2:T(8,128)S(1)} %collective-permute-done.22), channel_id=1, source_target_pairs={{0,2},{1,3},{2,0},{3,1},{4,6},{5,7},{6,4},{7,5},{8,10},{9,11},{10,... | collective-permute-start | bytes 27656 | tf_op jit(solution)/shard_map/ppermute | solution.py:26
  (24 other events, 624.4 us)
where the time goes:
time: 282 us
  blocking collectives  184 us (65%)
  starting transfers between devices  50.7 us (18%)
  local copies, waits for them, and re-layouts  15.3 us (5%)
  waiting for transfers between devices  13.8 us (5%)
  other arithmetic  9.88 us (4%)
  matrix products  5.9 us (2%)
    psum x3, blocking collectives, padded_tile(): summed_cols = lax.psum(cross_cols, 'tx')  116 us
    psum x3, blocking collectives, padded_tile(): row_block = lax.psum(col_sides, 'ty')  35 us
    psum x3, blocking collectives, padded_tile(): summed_rows = lax.psum(cross_rows, 'ty')  33.1 us
    ppermute x15, starting transfers between devices, partner(): return lax.ppermute(value, axis, pairs)  24.2 us
    ppermute x6, starting transfers between devices, extended(): before = lax.ppermute(last, axis, up)  18.7 us
    ppermute x15, waiting for transfers between devices, partner(): return lax.ppermute(value, axis, pairs)  11.6 us
    ppermute x6, starting transfers between devices, extended(): after = lax.ppermute(first, axis, down)  7.74 us
    gather x12, local copies, waits for them, and re-layouts, window_piece(): picked = jnp.take(held_block, jnp.clip(local_index, 0, length - 1), axis=2)  6.65 us
  transfers between devices with their start and end apart: 27, of which 10 were waited for; matrix products, arithmetic and copies ran while one was open for 5% of the time, Pallas kernels for 0%

commit v1 on v0

--- a/solution.py
+++ b/solution.py
@@ -115,7 +115,8 @@
             window_piece(row_block, side_cells - 1 - col_positions, row_index * tile_rows),
         ]
     )
-    summed_cols = lax.psum(cross_cols, "tx")
+    blocks = lax.all_gather(cross_cols, "tx")
+    summed_cols = jnp.sum(blocks, axis=0)
     cross_rows = jnp.stack(
         [
             window_piece(col_block, row_positions, col_index * tile_cols),

time: 282 us -> 353 us (1.25)
  blocking collectives: 184 us -> 245 us
  starting transfers between devices: 50.7 us -> 44.4 us
  other arithmetic: 9.88 us -> 16.1 us
  waiting for transfers between devices: 13.8 us -> 18 us
  local copies, waits for them, and re-layouts: 15.3 us -> 19.2 us
    all_gather x0 -> x3, blocking collectives: none -> 99.1 us  [padded_tile(): blocks = lax.all_gather(cross_cols, 'tx')]
    psum x6 -> x3, blocking collectives: 149 us -> 111 us  [padded_tile(): col_block = lax.psum(row_sides, 'tx')]
    ppermute x6, starting transfers between devices: 18.7 us -> 10.5 us  [extended(): before = lax.ppermute(last, axis, up)]
    ppermute x6, waiting for transfers between devices: 0.02 us -> 7.81 us  [extended(): after = lax.ppermute(first, axis, down)]
  transfers between devices with their start and end apart: 27 -> 27, of which waited for: 10 -> 8; matrix products, arithmetic and copies ran while one was open for 5% -> 6% of each run, Pallas kernels for 0% -> 0%
where the time goes in v1:
time: 353 us; the launch traced here: 352 us
  blocking collectives  245 us (69%)
  starting transfers between devices  44.4 us (13%)
  local copies, waits for them, and re-layouts  19.2 us (5%)
  waiting for transfers between devices  18 us (5%)
  other arithmetic  16.1 us (5%)
  matrix products  7.39 us (2%)
    psum x3, blocking collectives, padded_tile(): col_block = lax.psum(row_sides, 'tx')  111 us
    all_gather x3, blocking collectives, padded_tile(): blocks = lax.all_gather(cross_cols, 'tx')  99.1 us
    psum x3, blocking collectives, padded_tile(): row_block = lax.psum(col_sides, 'ty')  34.6 us
    ppermute x15, starting transfers between devices, partner(): return lax.ppermute(value, axis, pairs)  26.2 us
    ppermute x6, starting transfers between devices, extended(): before = lax.ppermute(last, axis, up)  10.5 us
    ppermute x15, waiting for transfers between devices, partner(): return lax.ppermute(value, axis, pairs)  10.1 us
    ppermute x6, waiting for transfers between devices, extended(): after = lax.ppermute(first, axis, down)  7.81 us
    ppermute x6, starting transfers between devices, extended(): after = lax.ppermute(first, axis, down)  7.75 us
  transfers between devices with their start and end apart: 27, of which 8 were waited for; matrix products, arithmetic and copies ran while one was open for 6% of the time, Pallas kernels for 0%

profile of v1, /device:TPU:0, one launch (start us, length us, event | category | flops | bytes accessed | tf_op | source)
XLA Modules:
  0.0 352.2 jit_solution(15026205470763318783)
XLA Ops:
  1.8 1.8 fusion.17
  4.4 39.8 %psum.63 = f32[2,6,12,16]{3,1,0,2:T(8,128)S(1)} all-reduce(f32[2,6,12,16]{3,1,0,2:T(8,128)S(1)} %copy.91), channel_id=1, replica_groups=mesh['tx'=8,'ty'=4] {'tx'}, use_global_device_ids=true, to_apply=%region_0.0 | all-reduce | flops 2304 | bytes 18432 | tf_op jit(solution)/shard_map/psum | solution.py:108
  45.8 11.7 %all-reduce.10 = (f32[2,6,6,16]{3,1,0,2:T(8,128)S(1)}, f32[2,2,6,6,16]{4,2,1,3,0:T(8,128)S(1)}) all-reduce(f32[2,6,6,16]{3,1,0,2:T(8,128)S(1)} %copy_multiply_fusion.3, f32[2,2,6,6,16]{4,2,1,3,0:T(8,128)S(1)} %pad_maximum_fusion.7), channel_id=1, replica_groups=mesh['tx'=8,'ty'=4] {'ty'}, use_global_device_ids=true, to_apply=%region_1.0 | all-reduce | flops 3456 | bytes 27648 | tf_op jit(solution)/shard_map/psum | solution.py:109
  59.1 3.6 %collective-permute-start = (f32[6,1,12,16]{3,0,2,1:T(8,128)}, f32[6,1,12,16]{3,0,2,1:T(8,128)S(1)}, u32[]{:S(2)}, u32[]{:S(2)}) collective-permute-start(f32[6,1,12,16]{3,0,2,1:T(8,128)} %get-tuple-element.195), channel_id=1, source_target_pairs={{0,4},{4,8},{8,12},{12,16},{16,20},{20,24},{24,28},{1,5},{5,9},{9,... | collective-permute-start | bytes 13832 | tf_op jit(solution)/shard_map/ppermute | solution.py:17
  69.1 34.1 %all-gather = f32[16,2,6,12,16]{4,1,3,2,0:T(2,128)S(1)} all-gather(f32[2,2,6,12,16]{4,1,3,2,0:T(2,128)S(1)} %copy.93), channel_id=2, replica_groups=mesh['tx'=8,'ty'=4] {'tx'}, dimensions={0}, use_global_device_ids=true | all-gather | bytes 165888 | tf_op jit(solution)/shard_map/all_gather | solution.py:118
  112.1 3.9 %collective-permute-done.7 = f32[2,6,6,16]{3,1,0,2:T(8,128)S(1)} collective-permute-done((f32[2,6,6,16]{3,1,0,2:T(8,128)}, f32[2,6,6,16]{3,1,0,2:T(8,128)S(1)}, u32[]{:S(2)}, u32[]{:S(2)}) %collective-permute-start.7) | collective-permute-done | bytes 4640 | tf_op jit(solution)/shard_map/ppermute | solution.py:26
  116.1 5.4 %collective-permute-start.5 = (f32[2,6,12,16]{3,1,0,2:T(8,128)}, f32[2,6,12,16]{3,1,0,2:T(8,128)S(1)}, u32[]{:S(2)}, u32[]{:S(2)}) collective-permute-start(f32[2,6,12,16]{3,1,0,2:T(8,128)} %collective-permute-done.4), channel_id=1, source_target_pairs={{0,2},{1,3},{2,0},{3,1},{4,6},{5,7},{6,4},{7,5},{8,10},{9,11},{10,... | collective-permute-start | bytes 27656 | tf_op jit(solution)/shard_map/ppermute | solution.py:26
  121.9 2.4 collective-permute-done.5
  127.7 35.0 %psum.66 = f32[2,6,6,16]{3,1,0,2:T(8,128)S(1)} all-reduce(f32[2,6,6,16]{3,1,0,2:T(8,128)S(1)} %copy.104), channel_id=1, replica_groups=mesh['tx'=8,'ty'=4] {'tx'}, use_global_device_ids=true, to_apply=%region_7.10 | all-reduce | flops 1152 | bytes 9216 | tf_op jit(solution)/shard_map/psum | solution.py:108
  164.0 11.2 %all-reduce.9 = (f32[2,6,3,16]{3,1,0,2:T(8,128)S(1)}, f32[2,2,6,3,16]{4,2,1,3,0:T(8,128)S(1)}) all-reduce(f32[2,6,3,16]{3,1,0,2:T(8,128)S(1)} %maximum_multiply_fusion.4, f32[2,2,6,3,16]{4,2,1,3,0:T(8,128)S(1)} %pad_maximum_fusion.11), channel_id=1, replica_groups=mesh['tx'=8,'ty'=4] {'ty'}, use_global_device_ids=true, to_apply=%region_8.11 | all-reduce | flops 1728 | bytes 13824 | tf_op jit(solution)/shard_map/psum | solution.py:109
  177.1 31.5 %all-gather.1 = f32[16,2,6,6,16]{4,1,3,2,0:T(2,128)S(1)} all-gather(f32[2,2,6,6,16]{4,1,3,2,0:T(2,128)S(1)} %copy.106), channel_id=3, replica_groups=mesh['tx'=8,'ty'=4] {'tx'}, dimensions={0}, use_global_device_ids=true | all-gather | bytes 82944 | tf_op jit(solution)/shard_map/all_gather | solution.py:118
  212.0 4.2 %collective-permute-done.10 = f32[6,1,6,16]{3,0,1,2:T(8,128)S(1)} collective-permute-done((f32[6,1,6,16]{3,0,1,2:T(8,128)S(1)}, f32[6,1,6,16]{3,0,1,2:T(8,128)S(1)}, u32[]{:S(2)}, u32[]{:S(2)}) %collective-permute-start.10) | collective-permute-done | bytes 2336 | tf_op jit(solution)/shard_map/ppermute | solution.py:18
  219.4 3.4 collective-permute-start.13
  222.8 3.5 collective-permute-start.17
  226.4 3.2 collective-permute-start.14
  230.0 1.7 collective-permute-done.14
  235.0 36.3 %psum.69 = f32[2,6,12,16]{3,1,2,0:T(8,128)S(1)} all-reduce(f32[2,6,12,16]{3,1,2,0:T(8,128)S(1)} %maximum_multiply_fusion.1), channel_id=1, replica_groups=mesh['tx'=8,'ty'=4] {'tx'}, use_global_device_ids=true, to_apply=%region_11.16 | all-reduce | flops 2304 | bytes 18432 | tf_op jit(solution)/shard_map/psum | solution.py:108
  273.0 11.7 %all-reduce.8 = (f32[2,6,6,16]{3,1,0,2:T(8,128)S(1)}, f32[2,2,6,6,16]{4,2,1,3,0:T(8,128)S(1)}) all-reduce(f32[2,6,6,16]{3,1,0,2:T(8,128)S(1)} %maximum_multiply_fusion.3, f32[2,2,6,6,16]{4,2,1,3,0:T(8,128)S(1)} %pad_maximum_fusion.9), channel_id=1, replica_groups=mesh['tx'=8,'ty'=4] {'ty'}, use_global_device_ids=true, to_apply=%region_12.17 | all-reduce | flops 3456 | bytes 27648 | tf_op jit(solution)/shard_map/psum | solution.py:109
  288.6 33.5 %all-gather.2 = f32[16,2,6,12,16]{4,1,3,2,0:T(2,128)S(1)} all-gather(f32[2,2,6,12,16]{4,1,3,2,0:T(2,128)S(1)} %copy.117), channel_id=4, replica_groups=mesh['tx'=8,'ty'=4] {'tx'}, dimensions={0}, use_global_device_ids=true | all-gather | bytes 165888 | tf_op jit(solution)/shard_map/all_gather | solution.py:118
  328.5 3.6 %collective-permute-done.19 = f32[6,1,12,16]{3,0,2,1:T(8,128)S(1)} collective-permute-done((f32[6,1,12,16]{3,0,2,1:T(8,128)}, f32[6,1,12,16]{3,0,2,1:T(8,128)S(1)}, u32[]{:S(2)}, u32[]{:S(2)}) %collective-permute-start.19) | collective-permute-done | bytes 4640 | tf_op jit(solution)/shard_map/ppermute | solution.py:18
  336.0 3.5 collective-permute-start.22
  339.5 3.5 collective-permute-start.26
  343.1 3.0 collective-permute-start.23
  346.8 1.9 collective-permute-done.23
  (294 shorter events, 56.6 us)
Async XLA Ops:
  58.1 53.5 %collective-permute-start.6 = (f32[2,6,6,16]{3,1,0,2:T(8,128)}, f32[2,6,6,16]{3,1,0,2:T(8,128)}, u32[]{:S(2)}, u32[]{:S(2)}) collective-permute-start(f32[2,6,6,16]{3,1,0,2:T(8,128)} %rev.19), channel_id=1, source_target_pairs={{0,4},{4,0},{8,12},{12,8},{16,20},{20,16},{24,28},{28,24},{1,5},{5... | collective-permute-start | bytes 13832 | tf_op jit(solution)/shard_map/ppermute | solution.py:26
  58.7 57.3 %collective-permute-start.4 = (f32[2,6,12,16]{3,1,0,2:T(8,128)}, f32[2,6,12,16]{3,1,0,2:T(8,128)}, u32[]{:S(2)}, u32[]{:S(2)}) collective-permute-start(f32[2,6,12,16]{3,1,0,2:T(8,128)} %rev.18), channel_id=1, source_target_pairs={{0,1},{1,0},{2,3},{3,2},{4,5},{5,4},{6,7},{7,6},{8,9},{9,8},{10,11... | collective-permute-start | bytes 27656 | tf_op jit(solution)/shard_map/ppermute | solution.py:26
  59.1 49.9 %collective-permute-start = (f32[6,1,12,16]{3,0,2,1:T(8,128)}, f32[6,1,12,16]{3,0,2,1:T(8,128)S(1)}, u32[]{:S(2)}, u32[]{:S(2)}) collective-permute-start(f32[6,1,12,16]{3,0,2,1:T(8,128)} %get-tuple-element.195), channel_id=1, source_target_pairs={{0,4},{4,8},{8,12},{12,16},{16,20},{20,24},{24,28},{1,5},{5,9},{9,... | collective-permute-start | bytes 13832 | tf_op jit(solution)/shard_map/ppermute | solution.py:17
  62.7 46.2 %collective-permute-start.1 = (f32[6,1,12,16]{3,0,1,2:T(8,128)S(1)}, f32[6,1,12,16]{3,0,1,2:T(8,128)S(1)}, u32[]{:S(2)}, u32[]{:S(2)}) collective-permute-start(f32[6,1,12,16]{3,0,1,2:T(8,128)S(1)} %get-tuple-element.194), channel_id=1, source_target_pairs={{4,0},{8,4},{12,8},{16,12},{20,16},{24,20},{28,24},{5,1},{9,5},{13... | collective-permute-start | bytes 13832 | tf_op jit(solution)/shard_map/ppermute | solution.py:18
  109.0 7.0 %collective-permute-start.2 = (f32[6,8,1,16]{3,0,1,2:T(8,128)S(1)}, f32[6,8,1,16]{3,0,1,2:T(8,128)S(1)}, u32[]{:S(2)}, u32[]{:S(2)}) collective-permute-start(f32[6,8,1,16]{3,0,1,2:T(8,128)S(1)} %get-tuple-element.180), channel_id=1, source_target_pairs={{0,1},{1,2},{2,3},{4,5},{5,6},{6,7},{8,9},{9,10},{10,11},{12,13},{... | collective-permute-start | bytes 9224 | tf_op jit(solution)/shard_map/ppermute | solution.py:17
  110.3 5.7 %collective-permute-start.3 = (f32[6,8,1,16]{3,0,1,2:T(8,128)S(1)}, f32[6,8,1,16]{3,0,1,2:T(8,128)S(1)}, u32[]{:S(2)}, u32[]{:S(2)}) collective-permute-start(f32[6,8,1,16]{3,0,1,2:T(8,128)S(1)} %get-tuple-element.181), channel_id=1, source_target_pairs={{1,0},{2,1},{3,2},{5,4},{6,5},{7,6},{9,8},{10,9},{11,10},{13,12},{... | collective-permute-start | bytes 9224 | tf_op jit(solution)/shard_map/ppermute | solution.py:18
  111.6 4.4 %collective-permute-start.7 = (f32[2,6,6,16]{3,1,0,2:T(8,128)}, f32[2,6,6,16]{3,1,0,2:T(8,128)S(1)}, u32[]{:S(2)}, u32[]{:S(2)}) collective-permute-start(f32[2,6,6,16]{3,1,0,2:T(8,128)} %collective-permute-done.6), channel_id=1, source_target_pairs={{0,8},{4,12},{8,0},{12,4},{16,24},{20,28},{24,16},{28,20},{1,9},{5... | collective-permute-start | bytes 13832 | tf_op jit(solution)/shard_map/ppermute | solution.py:26
  115.9 5.5 %collective-permute-start.8 = (f32[2,6,6,16]{3,1,0,2:T(8,128)S(1)}, f32[2,6,6,16]{3,1,0,2:T(8,128)S(1)}, u32[]{:S(2)}, u32[]{:S(2)}) collective-permute-start(f32[2,6,6,16]{3,1,0,2:T(8,128)S(1)} %collective-permute-done.7), channel_id=1, source_target_pairs={{0,16},{4,20},{8,24},{12,28},{16,0},{20,4},{24,8},{28,12},{1,17},{... | collective-permute-start | bytes 13832 | tf_op jit(solution)/shard_map/ppermute | solution.py:26
  116.1 8.2 %collective-permute-start.5 = (f32[2,6,12,16]{3,1,0,2:T(8,128)}, f32[2,6,12,16]{3,1,0,2:T(8,128)S(1)}, u32[]{:S(2)}, u32[]{:S(2)}) collective-permute-start(f32[2,6,12,16]{3,1,0,2:T(8,128)} %collective-permute-done.4), channel_id=1, source_target_pairs={{0,2},{1,3},{2,0},{3,1},{4,6},{5,7},{6,4},{7,5},{8,10},{9,11},{10,... | collective-permute-start | bytes 27656 | tf_op jit(solution)/shard_map/ppermute | solution.py:26
  175.7 43.2 %collective-permute-start.15 = (f32[2,6,3,16]{3,1,0,2:T(8,128)S(1)}, f32[2,6,3,16]{3,1,0,2:T(8,128)S(1)}, u32[]{:S(2)}, u32[]{:S(2)}) collective-permute-start(f32[2,6,3,16]{3,1,0,2:T(8,128)S(1)} %rev.21), channel_id=1, source_target_pairs={{0,4},{4,0},{8,12},{12,8},{16,20},{20,16},{24,28},{28,24},{1,5},{5... | collective-permute-start | bytes 6920 | tf_op jit(solution)/shard_map/ppermute | solution.py:26
  210.5 5.7 %collective-permute-start.10 = (f32[6,1,6,16]{3,0,1,2:T(8,128)S(1)}, f32[6,1,6,16]{3,0,1,2:T(8,128)S(1)}, u32[]{:S(2)}, u32[]{:S(2)}) collective-permute-start(f32[6,1,6,16]{3,0,1,2:T(8,128)S(1)} %get-tuple-element.214), channel_id=1, source_target_pairs={{4,0},{8,4},{12,8},{16,12},{20,16},{24,20},{28,24},{5,1},{9,5},{13... | collective-permute-start | bytes 6920 | tf_op jit(solution)/shard_map/ppermute | solution.py:18
  216.2 10.1 %collective-permute-start.11 = (f32[6,5,1,16]{3,0,1,2:T(8,128)S(1)}, f32[6,5,1,16]{3,0,1,2:T(8,128)S(1)}, u32[]{:S(2)}, u32[]{:S(2)}) collective-permute-start(f32[6,5,1,16]{3,0,1,2:T(8,128)S(1)} %get-tuple-element.202), channel_id=1, source_target_pairs={{0,1},{1,2},{2,3},{4,5},{5,6},{6,7},{8,9},{9,10},{10,11},{12,13},{... | collective-permute-start | bytes 5768 | tf_op jit(solution)/shard_map/ppermute | solution.py:17
  217.5 8.8 %collective-permute-start.12 = (f32[6,5,1,16]{3,0,1,2:T(8,128)S(1)}, f32[6,5,1,16]{3,0,1,2:T(8,128)S(1)}, u32[]{:S(2)}, u32[]{:S(2)}) collective-permute-start(f32[6,5,1,16]{3,0,1,2:T(8,128)S(1)} %get-tuple-element.203), channel_id=1, source_target_pairs={{1,0},{2,1},{3,2},{5,4},{6,5},{7,6},{9,8},{10,9},{11,10},{13,12},{... | collective-permute-start | bytes 5768 | tf_op jit(solution)/shard_map/ppermute | solution.py:18
  219.4 7.0 %collective-permute-start.13 = (f32[2,6,6,16]{3,1,0,2:T(8,128)S(1)}, f32[2,6,6,16]{3,1,0,2:T(8,128)S(1)}, u32[]{:S(2)}, u32[]{:S(2)}) collective-permute-start(f32[2,6,6,16]{3,1,0,2:T(8,128)S(1)} %rev.20), channel_id=1, source_target_pairs={{0,1},{1,0},{2,3},{3,2},{4,5},{5,4},{6,7},{7,6},{8,9},{9,8},{10,11... | collective-permute-start | bytes 13832 | tf_op jit(solution)/shard_map/ppermute | solution.py:26
  222.8 6.8 %collective-permute-start.17 = (f32[2,6,3,16]{3,1,0,2:T(8,128)S(1)}, f32[2,6,3,16]{3,1,0,2:T(8,128)S(1)}, u32[]{:S(2)}, u32[]{:S(2)}) collective-permute-start(f32[2,6,3,16]{3,1,0,2:T(8,128)S(1)} %collective-permute-done.16), channel_id=1, source_target_pairs={{0,16},{4,20},{8,24},{12,28},{16,0},{20,4},{24,8},{28,12},{1,17},{... | collective-permute-start | bytes 6920 | tf_op jit(solution)/shard_map/ppermute | solution.py:26
  226.4 5.3 %collective-permute-start.14 = (f32[2,6,6,16]{3,1,0,2:T(8,128)S(1)}, f32[2,6,6,16]{3,1,0,2:T(8,128)S(1)}, u32[]{:S(2)}, u32[]{:S(2)}) collective-permute-start(f32[2,6,6,16]{3,1,0,2:T(8,128)S(1)} %collective-permute-done.13), channel_id=1, source_target_pairs={{0,2},{1,3},{2,0},{3,1},{4,6},{5,7},{6,4},{7,5},{8,10},{9,11},{10,... | collective-permute-start | bytes 13832 | tf_op jit(solution)/shard_map/ppermute | solution.py:26
  288.3 46.4 %collective-permute-start.24 = (f32[2,6,6,16]{3,1,0,2:T(8,128)}, f32[2,6,6,16]{3,1,0,2:T(8,128)}, u32[]{:S(2)}, u32[]{:S(2)}) collective-permute-start(f32[2,6,6,16]{3,1,0,2:T(8,128)} %rev.23), channel_id=1, source_target_pairs={{0,4},{4,0},{8,12},{12,8},{16,20},{20,16},{24,28},{28,24},{1,5},{5... | collective-permute-start | bytes 13832 | tf_op jit(solution)/shard_map/ppermute | solution.py:26
  325.9 6.2 %collective-permute-start.19 = (f32[6,1,12,16]{3,0,2,1:T(8,128)}, f32[6,1,12,16]{3,0,2,1:T(8,128)S(1)}, u32[]{:S(2)}, u32[]{:S(2)}) collective-permute-start(f32[6,1,12,16]{3,0,2,1:T(8,128)} %get-tuple-element.186), channel_id=1, source_target_pairs={{4,0},{8,4},{12,8},{16,12},{20,16},{24,20},{28,24},{5,1},{9,5},{13... | collective-permute-start | bytes 13832 | tf_op jit(solution)/shard_map/ppermute | solution.py:18
  332.1 10.9 %collective-permute-start.20 = (f32[6,8,1,16]{3,0,1,2:T(8,128)S(1)}, f32[6,8,1,16]{3,0,1,2:T(8,128)S(1)}, u32[]{:S(2)}, u32[]{:S(2)}) collective-permute-start(f32[6,8,1,16]{3,0,1,2:T(8,128)S(1)} %get-tuple-element.178), channel_id=1, source_target_pairs={{0,1},{1,2},{2,3},{4,5},{5,6},{6,7},{8,9},{9,10},{10,11},{12,13},{... | collective-permute-start | bytes 9224 | tf_op jit(solution)/shard_map/ppermute | solution.py:17
  333.4 9.6 %collective-permute-start.21 = (f32[6,8,1,16]{3,0,1,2:T(8,128)S(1)}, f32[6,8,1,16]{3,0,1,2:T(8,128)S(1)}, u32[]{:S(2)}, u32[]{:S(2)}) collective-permute-start(f32[6,8,1,16]{3,0,1,2:T(8,128)S(1)} %get-tuple-element.179), channel_id=1, source_target_pairs={{1,0},{2,1},{3,2},{5,4},{6,5},{7,6},{9,8},{10,9},{11,10},{13,12},{... | collective-permute-start | bytes 9224 | tf_op jit(solution)/shard_map/ppermute | solution.py:18
  334.7 4.8 %collective-permute-start.25 = (f32[2,6,6,16]{3,1,0,2:T(8,128)}, f32[2,6,6,16]{3,1,0,2:T(8,128)S(1)}, u32[]{:S(2)}, u32[]{:S(2)}) collective-permute-start(f32[2,6,6,16]{3,1,0,2:T(8,128)} %collective-permute-done.24), channel_id=1, source_target_pairs={{0,8},{4,12},{8,0},{12,4},{16,24},{20,28},{24,16},{28,20},{1,9},{5... | collective-permute-start | bytes 13832 | tf_op jit(solution)/shard_map/ppermute | solution.py:26
  336.0 7.1 %collective-permute-start.22 = (f32[2,6,12,16]{3,1,2,0:T(8,128)S(1)}, f32[2,6,12,16]{3,1,2,0:T(8,128)S(1)}, u32[]{:S(2)}, u32[]{:S(2)}) collective-permute-start(f32[2,6,12,16]{3,1,2,0:T(8,128)S(1)} %rev.22), channel_id=1, source_target_pairs={{0,1},{1,0},{2,3},{3,2},{4,5},{5,4},{6,7},{7,6},{8,9},{9,8},{10,11... | collective-permute-start | bytes 27656 | tf_op jit(solution)/shard_map/ppermute | solution.py:26
  339.5 6.8 %collective-permute-start.26 = (f32[2,6,6,16]{3,1,0,2:T(8,128)S(1)}, f32[2,6,6,16]{3,1,0,2:T(8,128)S(1)}, u32[]{:S(2)}, u32[]{:S(2)}) collective-permute-start(f32[2,6,6,16]{3,1,0,2:T(8,128)S(1)} %collective-permute-done.25), channel_id=1, source_target_pairs={{0,16},{4,20},{8,24},{12,28},{16,0},{20,4},{24,8},{28,12},{1,17},{... | collective-permute-start | bytes 13832 | tf_op jit(solution)/shard_map/ppermute | solution.py:26
  343.1 5.6 %collective-permute-start.23 = (f32[2,6,12,16]{3,1,2,0:T(8,128)S(1)}, f32[2,6,12,16]{3,1,2,0:T(8,128)S(1)}, u32[]{:S(2)}, u32[]{:S(2)}) collective-permute-start(f32[2,6,12,16]{3,1,2,0:T(8,128)S(1)} %collective-permute-done.22), channel_id=1, source_target_pairs={{0,2},{1,3},{2,0},{3,1},{4,6},{5,7},{6,4},{7,5},{8,10},{9,11},{10,... | collective-permute-start | bytes 27656 | tf_op jit(solution)/shard_map/ppermute | solution.py:26
  (58 other events, 1614.7 us)
